TPU v7x, 512 devices: a whole 4x4x16 slice. The times are simulated.
512 devices in a mesh: dp: 8 (over z_hi, core), ctx: 64 (over x, z_lo, y).
Axes of the slice: x: 4, y: 4, z: 16 (z_hi: 4, z_lo: 4; z = z_hi * 4 + z_lo), core: 2. Of those that a mesh axis runs over, the one named last changes fastest.
Arguments:
- queries: bfloat16 [8, 2048, 8192], P('dp', None, 'ctx'), may hold values from -6 to 6
- keys: bfloat16 [8, 2048, 8192], P('dp', None, 'ctx'), may hold values from -6 to 6
- values: bfloat16 [8, 2048, 8192], P('dp', None, 'ctx'), may hold values from -6 to 6
- cotangent: bfloat16 [8, 2048, 8192], P('dp', None, 'ctx'), may hold values from -6 to 6
- residues: float32 [2048, 16], P(('dp', 'ctx')), may hold values from -1.5 to 1.5
- decays: float32 [2048, 16], P(('dp', 'ctx')), may hold values from 0.1 to 800
Outputs:
- mixed: bfloat16 [8, 2048, 8192], P('dp', None, 'ctx')
- grad_queries: bfloat16 [8, 2048, 8192], P('dp', None, 'ctx')
- grad_keys: bfloat16 [8, 2048, 8192], P('dp', None, 'ctx')
- grad_values: bfloat16 [8, 2048, 8192], P('dp', None, 'ctx')
- grad_residues: float32 [2048, 16], P(('dp', 'ctx'))
All inputs are finite; a program needn't handle non-finite values.
Results may differ from a plain program's by a relative error of at most 0.0057.
Values may be sent and summed in bfloat16 or wider, within the bound.
A program may use at most 64 MiB of HBM per device.

v0:
```python
import math
import jax
import jax.numpy as jnp
from jax import lax
from jax.sharding import PartitionSpec as P

exact_mode = lax.Precision.HIGHEST


def shift_along(x, axis, n, step):
    if step > 0:
        pairs = [(i, i + step) for i in range(n - step)]
    else:
        pairs = [(i, i + step) for i in range(-step, n)]
    return lax.ppermute(x, axis, perm=pairs)


def chunk_scan(state, chunk_decay, axis, n, direction):
    carry = shift_along(state, axis, n, direction)
    hop = 1
    while hop < n:
        carry = carry + jnp.exp(-chunk_decay * hop) * shift_along(carry, axis, n, direction * hop)
        hop *= 2
    return carry


def body(queries, keys, values, cotangent, residues, decays):
    n_dp = lax.axis_size("dp")
    n_ctx = lax.axis_size("ctx")
    seq_count, channels, chunk = keys.shape
    order = residues.shape[1]
    length = chunk * n_ctx
    f32 = jnp.float32
    params = lax.all_gather(
        jnp.concatenate([residues, decays], axis=1), ("dp", "ctx"), axis=0, tiled=True
    )
    dec = params[:, order:]
    scale = jnp.sqrt(1.0 - jnp.exp(-2.0 * dec / length))
    weight = params[:, :order] * scale
    gated_in = (keys.astype(f32) * values.astype(f32)).astype(jnp.bfloat16)
    gated_grad = (cotangent.astype(f32) * queries.astype(f32)).astype(jnp.bfloat16)
    g = gated_in[0].astype(f32)
    gg = gated_grad[0].astype(f32)
    pos = jnp.arange(chunk, dtype=f32)
    mid = chunk // 2
    dk = dec[:, :, None]
    grow = jnp.exp(dk * ((pos - mid) / length))
    shrink = jnp.exp(-dk * ((pos - mid) / length))
    upper = (pos[:, None] <= pos[None, :]).astype(f32)
    lower = (pos[:, None] >= pos[None, :]).astype(f32)
    end_fwd = jnp.sum(g[:, None, :] * jnp.exp(-dk * ((chunk - 1 - pos) / length)), axis=-1)
    start_bwd = jnp.sum(gg[:, None, :] * jnp.exp(-dk * (pos / length)), axis=-1)
    chunk_decay = dec * (chunk / length)
    carry_fwd = chunk_scan(end_fwd, chunk_decay, "ctx", n_ctx, 1)
    carry_bwd = chunk_scan(start_bwd, chunk_decay, "ctx", n_ctx, -1)
    fwd_state = shrink * jnp.einsum(
        "dnc,ct->dnt", g[:, None, :] * grow, upper, precision=exact_mode
    )
    bwd_state = grow * jnp.einsum(
        "dnc,ct->dnt", gg[:, None, :] * shrink, lower, precision=exact_mode
    )
    conv_intra = jnp.sum(weight[:, :, None] * fwd_state, axis=1)
    back_intra = jnp.sum(weight[:, :, None] * bwd_state, axis=1)
    cross_intra = jnp.sum(gg[:, None, :] * fwd_state, axis=-1)
    lead_fwd = jnp.exp(-dk * ((pos + 1) / length))
    lead_bwd = jnp.exp(-dk * ((chunk - pos) / length))
    conv_full = conv_intra + jnp.sum((weight * carry_fwd)[:, :, None] * lead_fwd, axis=1)
    back_full = back_intra + jnp.sum((weight * carry_bwd)[:, :, None] * lead_bwd, axis=1)
    cross = cross_intra + carry_fwd * jnp.sum(gg[:, None, :] * lead_fwd, axis=-1)
    total = lax.psum_scatter(cross, ("dp", "ctx"), scatter_dimension=0, tiled=True)
    own_scale = jnp.sqrt(1.0 - jnp.exp(-2.0 * decays / length))
    grad_residues = total * own_scale / math.sqrt(seq_count * n_dp * length)
    conv_f = conv_full.astype(jnp.bfloat16).astype(f32)[None]
    back_f = back_full.astype(jnp.bfloat16).astype(f32)[None]
    mixed = (queries.astype(f32) * conv_f).astype(jnp.bfloat16)
    grad_queries = (cotangent.astype(f32) * conv_f).astype(jnp.bfloat16)
    grad_keys = (back_f * values.astype(f32)).astype(jnp.bfloat16)
    grad_values = (back_f * keys.astype(f32)).astype(jnp.bfloat16)
    return (mixed, grad_queries, grad_keys, grad_values, grad_residues)


def solution(mesh):
    return jax.shard_map(
        body,
        mesh=mesh,
        in_specs=(
            P("dp", None, "ctx"),
            P("dp", None, "ctx"),
            P("dp", None, "ctx"),
            P("dp", None, "ctx"),
            P(("dp", "ctx"), None),
            P(("dp", "ctx"), None),
        ),
        out_specs=(
            P("dp", None, "ctx"),
            P("dp", None, "ctx"),
            P("dp", None, "ctx"),
            P("dp", None, "ctx"),
            P(("dp", "ctx"), None),
        ),
        check_vma=False,
    )
```

profile of v0, /device:TPU:1, one launch (start us, length us, event | category | flops | bytes accessed | tf_op | source)
XLA Modules:
  0.0 1972.8 jit_solution(14904116960434394480)
XLA Ops:
  8.0 1328.5 %all-gather = f32[512,4,32]{2,1,0:T(4,128)S(1)} all-gather(f32[1,4,32]{2,1,0:T(4,128)S(1)} %maximum_bitcast_fusion), channel_id=1, replica_groups=mesh['dp'=8,'ctx'=64] {'dp','ctx'}, dimensions={0}, use_global_device_ids=true | all-gather | bytes 262656 | tf_op jit(solution)/shard_map/all_gather | solution.py:34
  1338.6 3.0 multiply_reduce_fusion.6
  1343.0 1.9 collective-permute-done
  1344.9 3.8 collective-permute-start.1
  1348.7 1.9 collective-permute-done.1
  1350.7 4.1 collective-permute-start.2
  1354.8 1.9 collective-permute-done.2
  1356.8 3.5 collective-permute-start.3
  1360.3 1.9 collective-permute-done.3
  1362.2 3.5 collective-permute-start.4
  1367.7 3.5 collective-permute-start.5
  1373.2 4.3 collective-permute-start.6
  1379.2 1.7 fusion.30
  1380.9 27.1 %multiply_reduce_fusion = (f32[2048,16]{0,1:T(8,128)S(1)}, f32[2048,16]{0,1:T(8,128)S(1)}, f32[2048,128]{0,1:T(8,128)}, f32[2048,16]{0,1:T(8,128)S(1)}, f32[2048,128]{0,1:T(8,128)}) fusion(f32[2048,128]{0,1:T(8,128)} %fusion.22, f32[128]{0:T(128)S(1)} %get-tuple-element.33, f32[2048,16]{0,1:T(8,128)} %copy-done.9, f32[128]{0:T(128)S(1)} %get-tuple-element.32, ...), kind=kOutput, calls=%fused_computation | convolution fusion | flops 6508953600 | bytes 5113344 | tf_op jit(solution)/shard_map/dnc,ct->dnt/dot_general | solution.py:56
  1409.5 4.4 collective-permute-done.7
  1415.2 4.4 collective-permute-done.8
  1419.6 1.6 multiply_add_fusion
  1422.5 6.2 collective-permute-done.9
  1431.1 17.7 multiply_reduce_fusion.4
  1450.4 5.1 collective-permute-done.11
  1460.3 3.4 collective-permute-done.12
  1463.8 1.5 collective-permute-start.13
  1465.3 493.2 %all-reduce.3.cloned.1.call-done = f32[2048,16]{1,0:T(8,128)} async-done(((f32[2048,16]{1,0:T(8,128)}), f32[2048,16]{1,0:T(8,128)}) %all-reduce.3.cloned.1.call-update) | async-done | bytes 131088
  1960.8 2.8 multiply_reduce_fusion.2
  (73 shorter events, 27.4 us)
Async XLA Ops:
  7.2 1951.4 %all-reduce.3.cloned.1.call-start = ((), (), s32[]{:S(2)}) async-start(), calls=%async_computation | async-start | bytes 2097152
  1338.6 3.0 copy-start.3
  1341.6 24.2 %copy-start.7 = (bf16[1,2048,128]{2,1,0:T(8,128)(2,1)S(1)}, bf16[1,2048,128]{2,1,0:T(8,128)(2,1)}, u32[]{:S(2)}) copy-start(bf16[1,2048,128]{2,1,0:T(8,128)(2,1)} %param.9) | copy-start | bytes 1572868
  1341.6 3.4 collective-permute-start
  1344.9 5.7 collective-permute-start.1
  1350.7 6.0 collective-permute-start.2
  1356.8 5.4 collective-permute-start.3
  1362.2 5.4 collective-permute-start.4
  1367.7 5.4 collective-permute-start.5
  1373.2 6.0 collective-permute-start.6
  1379.2 28.8 %copy-start.8 = (f32[2048,16]{0,1:T(8,128)}, f32[2048,16]{0,1:T(8,128)S(1)}, u32[]{:S(2)}) copy-start(f32[2048,16]{0,1:T(8,128)S(1)} %collective-permute-done.6) | copy-start | bytes 393220
  1408.1 23.0 %copy-start.4 = (f32[2048,128]{0,1:T(8,128)S(1)}, f32[2048,128]{0,1:T(8,128)}, u32[]{:S(2)}) copy-start(f32[2048,128]{0,1:T(8,128)} %fusion.22) | copy-start | bytes 3145732
  1408.1 5.8 collective-permute-start.7
  1413.9 5.7 collective-permute-start.8
  1421.2 7.5 collective-permute-start.9
  1429.8 19.0 collective-permute-start.10
  1431.1 19.0 copy-start.1
  1431.1 19.0 copy-start.2
  1448.8 6.6 collective-permute-start.11
  1455.5 8.3 collective-permute-start.12
  1460.3 498.3 %copy-start.11 = (f32[4,16]{1,0:T(4,128)S(1)}, f32[4,16]{1,0:T(4,128)}, u32[]{:S(2)}) copy-start(f32[4,16]{1,0:T(4,128)} %param.11) | copy-start | bytes 772
  1460.3 500.5 %copy-start.10 = (f32[2048,16]{0,1:T(8,128)S(1)}, f32[2048,16]{0,1:T(8,128)}, u32[]{:S(2)}) copy-start(f32[2048,16]{0,1:T(8,128)} %copy-done.9) | copy-start | bytes 393220
  1463.8 496.0 %collective-permute-start.13 = (f32[2048,16]{0,1:T(8,128)S(1)}, f32[2048,16]{0,1:T(8,128)S(1)}, u32[]{:S(2)}, u32[]{:S(2)}) collective-permute-start(f32[2048,16]{0,1:T(8,128)S(1)} %multiply_add_fusion.1), channel_id=1, source_target_pairs={{32,0},{33,1},{34,2},{35,3},{36,4},{37,5},{38,6},{39,7},{40,8},{41... | collective-permute-start | bytes 393224 | tf_op jit(solution)/shard_map/ppermute | solution.py:15
  1960.8 2.8 copy-start
  (3 other events, 2.8 us)
Sparse Core Ops, SparseCore 0:
  1460.4 498.0 all-reduce.2
where the time goes:
time: 1970 us
  blocking collectives  1330 us (68%)
  waiting for transfers between devices  526 us (27%)
  matrix products  44.8 us (2%)
  starting transfers between devices  33.5 us (2%)
    all_gather x1, blocking collectives, body(): lax.all_gather(jnp.concatenate([residues, decays], axis=1), ('dp', 'ctx')...  1330 us
    unnamed x2, waiting for transfers between devices  493 us
  transfers between devices with their start and end apart: 15, of which 13 were waited for; matrix products, arithmetic and copies ran while one was open for 1% of the time, Pallas kernels for 0%

commit v1 on v0

--- a/solution.py
+++ b/solution.py
@@ -31,8 +31,14 @@
     order = residues.shape[1]
     length = chunk * n_ctx
     f32 = jnp.float32
-    params = lax.all_gather(
-        jnp.concatenate([residues, decays], axis=1), ("dp", "ctx"), axis=0, tiled=True
+    params = jnp.concatenate(
+        lax.all_to_all(
+            jnp.stack([jnp.concatenate([residues, decays], axis=1)] * lax.axis_size(("dp", "ctx"))),
+            ("dp", "ctx"),
+            0,
+            0,
+        ),
+        axis=0,
     )
     dec = params[:, order:]
     scale = jnp.sqrt(1.0 - jnp.exp(-2.0 * dec / length))

time: 1970 us -> 709 us (0.36)
  blocking collectives: 1330 us -> 0 us
  starting transfers between devices: 33.5 us -> 80.5 us
    all_gather x1 -> x0, blocking collectives: 1330 us -> none  [body(): lax.all_gather(jnp.concatenate([residues, decays], axis=1), ('dp', 'ctx')...]
    all_to_all x0 -> x1, starting transfers between devices: none -> 24.3 us  [body(): lax.all_to_all(jnp.stack([jnp.concatenate([residues, decays], axis=1)] *...]
    all_to_all x0 -> x1, waiting for transfers between devices: none -> 22.8 us  [body(): lax.all_to_all(jnp.stack([jnp.concatenate([residues, decays], axis=1)] *...]
    ppermute x14, starting transfers between devices: 33.5 us -> 56.2 us  [shift_along(): return lax.ppermute(x, axis, perm=pairs)]
  transfers between devices with their start and end apart: 15 -> 16, of which waited for: 13 -> 14; matrix products, arithmetic and copies ran while one was open for 1% -> 4% of each run, Pallas kernels for 0% -> 0%
where the time goes in v1:
time: 709 us
  waiting for transfers between devices  539 us (76%)
  starting transfers between devices  80.5 us (11%)
  matrix products  44.8 us (6%)
  other arithmetic  16.1 us (2%)
  between operations  14.5 us (2%)
  local copies, waits for them, and re-layouts  14.3 us (2%)
    unnamed x2, waiting for transfers between devices  480 us
    ppermute x14, starting transfers between devices, shift_along(): return lax.ppermute(x, axis, perm=pairs)  56.2 us
    ppermute x14, waiting for transfers between devices, shift_along(): return lax.ppermute(x, axis, perm=pairs)  35.5 us
    dot_general x1, matrix products, body(): jnp.einsum('dnc,ct->dnt', g[:, None, :] * grow, upper, precision=exact_mode)  27.1 us
    all_to_all x1, starting transfers between devices, body(): lax.all_to_all(jnp.stack([jnp.concatenate([residues, decays], axis=1)] *...  24.3 us
    all_to_all x1, waiting for transfers between devices, body(): lax.all_to_all(jnp.stack([jnp.concatenate([residues, decays], axis=1)] *...  22.8 us
    dot_general x1, matrix products, body(): jnp.einsum('dnc,ct->dnt', gg[:, None, :] * shrink, lower, precision=exact...  17.7 us
  transfers between devices with their start and end apart: 16, of which 14 were waited for; matrix products, arithmetic and copies ran while one was open for 4% of the time, Pallas kernels for 0%

profile of v1, /device:TPU:1, one launch (start us, length us, event | category | flops | bytes accessed | tf_op | source)
XLA Modules:
  0.0 708.7 jit_solution(12483365844610787434)
XLA Ops:
  9.5 24.3 %all-to-all-start = ((f32[512,1,128]{2,1,0:T(1,128)}), f32[512,1,128]{2,1,0:T(1,128)S(1)}, u32[]{:S(2)}, u32[]{:S(2)}) async-start(f32[512,1,128]{2,1,0:T(1,128)} %reshape.108), calls=%async_computation | async-start | bytes 524288 | tf_op jit(solution)/shard_map/all_to_all | solution.py:35
  35.4 22.8 %all-to-all-done = f32[512,1,128]{2,1,0:T(1,128)S(1)} async-done(((f32[512,1,128]{2,1,0:T(1,128)}), f32[512,1,128]{2,1,0:T(1,128)S(1)}, u32[]{:S(2)}, u32[]{:S(2)}) %all-to-all-start) | async-done | bytes 262176 | tf_op jit(solution)/shard_map/all_to_all | solution.py:35
  63.4 3.0 multiply_reduce_fusion.6
  67.8 1.9 collective-permute-done
  69.8 3.8 collective-permute-start.1
  73.5 1.9 collective-permute-done.1
  75.5 5.5 collective-permute-start.2
  81.0 1.9 collective-permute-done.2
  83.0 10.9 %collective-permute-start.3 = (f32[2048,16]{0,1:T(8,128)S(1)}, f32[2048,16]{0,1:T(8,128)S(1)}, u32[]{:S(2)}, u32[]{:S(2)}) collective-permute-start(f32[2048,16]{0,1:T(8,128)S(1)} %multiply_add_fusion.10), channel_id=1, source_target_pairs={{0,4},{1,5},{2,6},{3,7},{4,8},{5,9},{6,10},{7,11},{8,12},{9,13},{1... | collective-permute-start | bytes 393224 | tf_op jit(solution)/shard_map/ppermute | solution.py:15
  93.9 1.9 collective-permute-done.3
  95.9 3.7 collective-permute-start.4
  101.5 14.8 %collective-permute-start.5 = (f32[2048,16]{0,1:T(8,128)S(1)}, f32[2048,16]{0,1:T(8,128)S(1)}, u32[]{:S(2)}, u32[]{:S(2)}) collective-permute-start(f32[2048,16]{0,1:T(8,128)S(1)} %multiply_add_fusion.8), channel_id=1, source_target_pairs={{0,16},{1,17},{2,18},{3,19},{4,20},{5,21},{6,22},{7,23},{8,24},{9,... | collective-permute-start | bytes 393224 | tf_op jit(solution)/shard_map/ppermute | solution.py:15
  118.2 6.8 collective-permute-start.6
  126.0 2.1 collective-permute-done.6
  129.8 27.1 %multiply_reduce_fusion = (f32[2048,16]{0,1:T(8,128)S(1)}, f32[2048,16]{0,1:T(8,128)S(1)}, f32[2048,128]{0,1:T(8,128)}, f32[2048,16]{0,1:T(8,128)S(1)}, f32[2048,128]{0,1:T(8,128)}) fusion(f32[2048,128]{0,1:T(8,128)} %fusion.22, f32[128]{0:T(128)S(1)} %get-tuple-element.33, f32[2048,16]{0,1:T(8,128)} %copy-done.11, f32[128]{0:T(128)S(1)} %get-tuple-element.32, ...), kind=kOutput, calls=%fused_computation | convolution fusion | flops 6508953600 | bytes 5113344 | tf_op jit(solution)/shard_map/dnc,ct->dnt/dot_general | solution.py:62
  158.3 4.4 collective-permute-done.7
  164.0 4.4 collective-permute-done.8
  168.4 1.6 multiply_add_fusion
  171.3 6.2 collective-permute-done.9
  179.9 17.7 %multiply_reduce_fusion.4 = f32[2048,128]{0,1:T(8,128)} fusion(f32[2048,16]{0,1:T(8,128)S(1)} %copy.52, f32[128]{0:T(128)S(1)} %add_multiply_fusion.2, f32[2048,16]{0,1:T(8,128)} %copy-done.8, f32[2048,128]{0,1:T(8,128)S(1)} %copy-done.4, f32[2048,16]{0,1:T(8,128)} %copy-done.11), kind=kOutput, calls=%fused_computation.4 | convolution fusion | flops 6467371008 | bytes 2490880 | tf_op jit(solution)/shard_map/dnc,ct->dnt/dot_general | solution.py:65
  199.2 5.1 collective-permute-done.11
  209.1 4.4 collective-permute-done.12
  215.0 480.3 %all-reduce.3.cloned.1.call-done = f32[2048,16]{1,0:T(8,128)} async-done(((f32[2048,16]{1,0:T(8,128)}), f32[2048,16]{1,0:T(8,128)}) %all-reduce.3.cloned.1.call-update) | async-done | bytes 131088
  696.7 2.8 multiply_reduce_fusion.2
  (83 shorter events, 35.1 us)
Async XLA Ops:
  8.1 25.8 %copy-start.5 = (bf16[1,2048,128]{2,1,0:T(8,128)(2,1)S(1)}, bf16[1,2048,128]{2,1,0:T(8,128)(2,1)}, u32[]{:S(2)}) copy-start(bf16[1,2048,128]{2,1,0:T(8,128)(2,1)} %param.8) | copy-start | bytes 1572868
  9.5 24.6 %copy-start.6 = (bf16[1,2048,128]{2,1,0:T(8,128)(2,1)S(1)}, bf16[1,2048,128]{2,1,0:T(8,128)(2,1)}, u32[]{:S(2)}) copy-start(bf16[1,2048,128]{2,1,0:T(8,128)(2,1)} %param.7) | copy-start | bytes 1572868
  9.5 48.7 %all-to-all-start = ((f32[512,1,128]{2,1,0:T(1,128)}), f32[512,1,128]{2,1,0:T(1,128)S(1)}, u32[]{:S(2)}, u32[]{:S(2)}) async-start(f32[512,1,128]{2,1,0:T(1,128)} %reshape.108), calls=%async_computation | async-start | bytes 524288 | tf_op jit(solution)/shard_map/all_to_all | solution.py:35
  33.8 661.6 %all-reduce.3.cloned.1.call-start = ((), (), s32[]{:S(2)}) async-start(), calls=%async_computation.1 | async-start | bytes 2097152
  66.4 33.2 %copy-start.7 = (bf16[1,2048,128]{2,1,0:T(8,128)(2,1)S(1)}, bf16[1,2048,128]{2,1,0:T(8,128)(2,1)}, u32[]{:S(2)}) copy-start(bf16[1,2048,128]{2,1,0:T(8,128)(2,1)} %param.9) | copy-start | bytes 1572868
  66.4 3.4 collective-permute-start
  69.8 5.7 collective-permute-start.1
  75.5 7.5 %collective-permute-start.2 = (f32[2048,16]{0,1:T(8,128)S(1)}, f32[2048,16]{0,1:T(8,128)S(1)}, u32[]{:S(2)}, u32[]{:S(2)}) collective-permute-start(f32[2048,16]{0,1:T(8,128)S(1)} %multiply_add_fusion.11), channel_id=1, source_target_pairs={{0,2},{1,3},{2,4},{3,5},{4,6},{5,7},{6,8},{7,9},{8,10},{9,11},{10,... | collective-permute-start | bytes 393224 | tf_op jit(solution)/shard_map/ppermute | solution.py:15
  83.0 12.8 %collective-permute-start.3 = (f32[2048,16]{0,1:T(8,128)S(1)}, f32[2048,16]{0,1:T(8,128)S(1)}, u32[]{:S(2)}, u32[]{:S(2)}) collective-permute-start(f32[2048,16]{0,1:T(8,128)S(1)} %multiply_add_fusion.10), channel_id=1, source_target_pairs={{0,4},{1,5},{2,6},{3,7},{4,8},{5,9},{6,10},{7,11},{8,12},{9,13},{1... | collective-permute-start | bytes 393224 | tf_op jit(solution)/shard_map/ppermute | solution.py:15
  95.9 5.6 collective-permute-start.4
  101.5 16.7 %collective-permute-start.5 = (f32[2048,16]{0,1:T(8,128)S(1)}, f32[2048,16]{0,1:T(8,128)S(1)}, u32[]{:S(2)}, u32[]{:S(2)}) collective-permute-start(f32[2048,16]{0,1:T(8,128)S(1)} %multiply_add_fusion.8), channel_id=1, source_target_pairs={{0,16},{1,17},{2,18},{3,19},{4,20},{5,21},{6,22},{7,23},{8,24},{9,... | collective-permute-start | bytes 393224 | tf_op jit(solution)/shard_map/ppermute | solution.py:15
  118.2 9.8 %collective-permute-start.6 = (f32[2048,16]{0,1:T(8,128)S(1)}, f32[2048,16]{0,1:T(8,128)S(1)}, u32[]{:S(2)}, u32[]{:S(2)}) collective-permute-start(f32[2048,16]{0,1:T(8,128)S(1)} %multiply_add_fusion.7), channel_id=1, source_target_pairs={{0,32},{1,33},{2,34},{3,35},{4,36},{5,37},{6,38},{7,39},{8,40},{9,... | collective-permute-start | bytes 393224 | tf_op jit(solution)/shard_map/ppermute | solution.py:15
  128.1 28.8 %copy-start.10 = (f32[2048,16]{0,1:T(8,128)}, f32[2048,16]{0,1:T(8,128)S(1)}, u32[]{:S(2)}) copy-start(f32[2048,16]{0,1:T(8,128)S(1)} %collective-permute-done.6) | copy-start | bytes 393220
  156.8 23.0 %copy-start.4 = (f32[2048,128]{0,1:T(8,128)S(1)}, f32[2048,128]{0,1:T(8,128)}, u32[]{:S(2)}) copy-start(f32[2048,128]{0,1:T(8,128)} %fusion.22) | copy-start | bytes 3145732
  156.8 5.8 collective-permute-start.7
  162.7 5.7 collective-permute-start.8
  170.0 7.5 %collective-permute-start.9 = (f32[2048,16]{0,1:T(8,128)}, f32[2048,16]{0,1:T(8,128)}, u32[]{:S(2)}, u32[]{:S(2)}) collective-permute-start(f32[2048,16]{0,1:T(8,128)} %get-tuple-element.31), channel_id=1, source_target_pairs={{2,0},{3,1},{4,2},{5,3},{6,4},{7,5},{8,6},{9,7},{10,8},{11,9},{12,... | collective-permute-start | bytes 393224 | tf_op jit(solution)/shard_map/ppermute | solution.py:15
  178.5 19.0 %collective-permute-start.10 = (f32[2048,16]{0,1:T(8,128)S(1)}, f32[2048,16]{0,1:T(8,128)S(1)}, u32[]{:S(2)}, u32[]{:S(2)}) collective-permute-start(f32[2048,16]{0,1:T(8,128)S(1)} %multiply_add_fusion.4), channel_id=1, source_target_pairs={{4,0},{5,1},{6,2},{7,3},{8,4},{9,5},{10,6},{11,7},{12,8},{13,9},{1... | collective-permute-start | bytes 393224 | tf_op jit(solution)/shard_map/ppermute | solution.py:15
  197.6 6.6 collective-permute-start.11
  204.2 9.2 %collective-permute-start.12 = (f32[2048,16]{0,1:T(8,128)S(1)}, f32[2048,16]{0,1:T(8,128)S(1)}, u32[]{:S(2)}, u32[]{:S(2)}) collective-permute-start(f32[2048,16]{0,1:T(8,128)S(1)} %multiply_add_fusion.2), channel_id=1, source_target_pairs={{16,0},{17,1},{18,2},{19,3},{20,4},{21,5},{22,6},{23,7},{24,8},{25... | collective-permute-start | bytes 393224 | tf_op jit(solution)/shard_map/ppermute | solution.py:15
  209.0 486.3 %copy-start.13 = (f32[4,16]{1,0:T(4,128)S(1)}, f32[4,16]{1,0:T(4,128)}, u32[]{:S(2)}) copy-start(f32[4,16]{1,0:T(4,128)} %param.11) | copy-start | bytes 772
  209.0 487.6 %copy-start.9 = (f32[2048,16]{0,1:T(8,128)S(1)}, f32[2048,16]{0,1:T(8,128)}, u32[]{:S(2)}) copy-start(f32[2048,16]{0,1:T(8,128)} %copy-done.8) | copy-start | bytes 393220
  209.0 487.7 %copy-start.12 = (f32[2048,16]{0,1:T(8,128)S(1)}, f32[2048,16]{0,1:T(8,128)}, u32[]{:S(2)}) copy-start(f32[2048,16]{0,1:T(8,128)} %copy-done.11) | copy-start | bytes 393220
  213.5 483.1 %collective-permute-start.13 = (f32[2048,16]{0,1:T(8,128)S(1)}, f32[2048,16]{0,1:T(8,128)S(1)}, u32[]{:S(2)}, u32[]{:S(2)}) collective-permute-start(f32[2048,16]{0,1:T(8,128)S(1)} %multiply_add_fusion.1), channel_id=1, source_target_pairs={{32,0},{33,1},{34,2},{35,3},{36,4},{37,5},{38,6},{39,7},{40,8},{41... | collective-permute-start | bytes 393224 | tf_op jit(solution)/shard_map/ppermute | solution.py:15
  (6 other events, 46.2 us)
Sparse Core Ops, SparseCore 0:
  209.2 486.1 all-reduce.2
